TPU v7x, 32 devices: a whole 2x2x4 slice. The times are simulated.
32 devices in a mesh: blk: 8 (over z, y), aux: 4 (over x, core).
Axes of the slice: x: 2, y: 2, z: 4, core: 2. Of those that a mesh axis runs over, the one named last changes fastest.
Arguments:
- adjoint: bfloat16 [1024, 1024], P(('blk', 'aux')), may hold values from -0.1875 to 0.1875
- three_centre: bfloat16 [128, 32, 32, 1024], P(('blk', 'aux')), may hold values from -1 to 1
- occ_density: bfloat16 [64, 1024], P('blk'), may hold values from -1 to 1
- vir_density: bfloat16 [64, 1024], P('blk'), may hold values from -1 to 1
- block_sizes: int32 [64], P('blk'), may hold values from 16 to 32
- tile_rows: int32 [128], P(('blk', 'aux')), may hold values from 0 to 7
- col_owner: int32 [128, 1], P(('blk', 'aux')), may hold values from 0 to 7; in each aligned block of 16 rows (0 to 15, 16 to 31, ...) at most 4 rows name the same one
- col_block: int32 [128], P(('blk', 'aux')), may hold values from 0 to 7
Outputs:
- occ_grad: float32 [64, 1024], P(('blk', 'aux'))
- vir_grad: float32 [64, 1024], P(('blk', 'aux'))
Inputs may be any that keep to these rules, and one draw needn't show every extreme that they name: `col_owner`: among the 16 tiles of one blk index (aligned blocks of 16 tiles), at most 4 name the same owner, and some blk index reaches 4.
All inputs are finite; a program needn't handle non-finite values.
Results may differ from a plain program's by a relative error of at most 0.0041.
Values may be sent and summed in bfloat16 or wider, within the bound.
A program may use at most 128 MiB of HBM per device.

v0:
```python
import functools

import jax
import jax.numpy as jnp
from jax import lax
from jax.experimental import pallas as pl
from jax.experimental.pallas import tpu as pltpu
from jax.sharding import PartitionSpec as P

BS = 32
CHUNK = 256
MESH = pl.DeviceIdType.MESH
F32 = jnp.float32
BF16 = jnp.bfloat16


def iota(shape, dim):
    return lax.broadcasted_iota(jnp.int32, shape, dim)


def gather_kernel(depth, pay_ref, out_ref, send_sem, recv_sem, own_sem):
    b = lax.axis_index("blk")
    a = lax.axis_index("aux")
    z, y, x, c = b // 2, b % 2, a // 2, a % 2
    up, down, over_x, over_y, mate = range(5)
    place = {
        up: (b + 2, a),
        down: (b - 2, a),
        over_x: (b, (1 - x) * 2 + c),
        over_y: (z * 2 + 1 - y, a),
        mate: (b, x * 2 + 1 - c),
    }
    has_up, has_down = z < depth - 1, z > 0

    def ident(xx, yy, zz, cc):
        return ((zz * 2 + yy) * 2 + xx) * 2 + cc

    me = ident(x, y, z, c)
    barrier = pltpu.get_barrier_semaphore()
    for way in (over_x, over_y, mate):
        pl.semaphore_signal(barrier, inc=1, device_id=place[way], device_id_type=MESH)

    @pl.when(has_up)
    def _():
        pl.semaphore_signal(barrier, inc=1, device_id=place[up], device_id_type=MESH)

    @pl.when(has_down)
    def _():
        pl.semaphore_signal(barrier, inc=1, device_id=place[down], device_id_type=MESH)

    own = pltpu.make_async_copy(pay_ref, out_ref.at[me], own_sem)
    own.start()
    pl.semaphore_wait(barrier, 3 + has_up.astype(jnp.int32) + has_down.astype(jnp.int32))

    def copy(way, block, src=None):
        return pltpu.make_async_remote_copy(
            src_ref=out_ref.at[block] if src is None else src,
            dst_ref=out_ref.at[block],
            send_sem=send_sem.at[way, block],
            recv_sem=recv_sem.at[block],
            device_id=place[way],
            device_id_type=MESH,
        )

    def send(way, block, src=None, when=None):
        if when is None:
            copy(way, block, src).start()
        else:

            @pl.when(when)
            def _():
                copy(way, block, src).start()

    def arrive(block):
        copy(mate, block).wait_recv()

    send(up, me, pay_ref, has_up)
    send(down, me, pay_ref, has_down)
    send(over_x, me, pay_ref)
    send(over_y, me, pay_ref)
    send(mate, me, pay_ref)

    def column(zz, from_up):
        block = ident(x, y, zz, c)
        arrive(block)
        if from_up:
            send(down, block, when=has_down)
        else:
            send(up, block, when=has_up)
        send(over_x, block)
        send(over_y, block)
        send(mate, block)

    def sides(zz):
        block = ident(1 - x, y, zz, c)
        arrive(block)
        send(over_y, block, when=zz % 2 == 0)
        send(mate, block)
        block = ident(x, 1 - y, zz, c)
        arrive(block)
        send(over_x, block, when=zz % 2 == 1)
        send(mate, block)

    def corner(zz):
        block = ident(1 - x, 1 - y, zz, c)
        arrive(block)
        send(mate, block)

    def planes(dist, work):
        if dist == 0:
            work(z, None)
        elif 0 < dist < depth:

            @pl.when(z + dist < depth)
            def _():
                work(z + dist, True)

            @pl.when(z - dist >= 0)
            def _():
                work(z - dist, False)

    for step in range(1, depth + 2):
        planes(step, column)
        planes(step - 1, lambda zz, _: sides(zz))
        if step >= 2:
            planes(step - 2, lambda zz, _: corner(zz))

    own.wait()
    for zz in range(depth):
        for xx in (x, 1 - x):
            for yy in (y, 1 - y):
                arrive(ident(xx, yy, zz, 1 - c))
    for zz in range(depth):
        block = ident(x, y, zz, c)
        for way in (over_x, over_y, mate):
            copy(way, block).wait_send()

        @pl.when((zz <= z) & has_up)
        def _():
            copy(up, ident(x, y, zz, c)).wait_send()

        @pl.when((zz >= z) & has_down)
        def _():
            copy(down, ident(x, y, zz, c)).wait_send()

        block = ident(1 - x, y, zz, c)
        copy(mate, block).wait_send()
        if zz % 2 == 0:
            copy(over_y, block).wait_send()
        block = ident(x, 1 - y, zz, c)
        copy(mate, block).wait_send()
        if zz % 2 == 1:
            copy(over_x, block).wait_send()
        copy(mate, ident(1 - x, 1 - y, zz, c)).wait_send()


def gather(payload, n_blk, n_aux):
    n_dev = n_blk * n_aux
    if n_aux != 4 or n_blk % 2:
        return lax.all_gather(payload, ("blk", "aux"), axis=0)
    return pl.pallas_call(
        functools.partial(gather_kernel, n_blk // 2),
        out_shape=jax.ShapeDtypeStruct((n_dev,) + payload.shape, payload.dtype),
        in_specs=[pl.BlockSpec(memory_space=pltpu.VMEM)],
        out_specs=pl.BlockSpec(memory_space=pltpu.VMEM),
        scratch_shapes=[
            pltpu.SemaphoreType.DMA((5, n_dev)),
            pltpu.SemaphoreType.DMA((n_dev,)),
            pltpu.SemaphoreType.DMA,
        ],
        compiler_params=pltpu.CompilerParams(collective_id=0, has_side_effects=True),
        name="gather",
    )(payload)


def tile_kernel(
    n_aux, own, sizes, rows, owners, blocks, occ_ref, vir_ref, adj_ref, t_ref, occ_out, vir_out, vir_acc
):
    t = pl.program_id(0)
    pairs = BS * BS
    naux = adj_ref.shape[0]

    @pl.when(t == 0)
    def _():
        occ_out[...] = jnp.zeros_like(occ_out)
        vir_acc[...] = jnp.zeros_like(vir_acc)

    row, owner, block = rows[t], owners[t], blocks[t]
    size = sizes[row]
    lane = iota((1, pairs), 1)
    inside = (lane // BS < size) & (lane % BS < size)
    occ_all = occ_ref[...].astype(F32)
    occ_row = jnp.sum(jnp.where(iota(occ_all.shape, 0) == row, occ_all, 0.0), axis=0, keepdims=True)
    occ_row = jnp.where(inside, occ_row, 0.0)
    home = owner * n_aux + block // own
    vir_all = vir_ref[home].astype(F32)
    vir_row = jnp.sum(jnp.where(iota(vir_all.shape, 0) == block % own, vir_all, 0.0), axis=0, keepdims=True)
    diag = iota((BS, pairs), 1) // BS == iota((BS, pairs), 0)
    fold_minor = (iota((pairs, 128), 0) % BS == iota((pairs, 128), 1) % BS).astype(BF16)
    fold_major = (iota((pairs, 128), 0) // BS == iota((pairs, 128), 1) % BS).astype(BF16)
    spread = (iota((128, pairs), 0) == iota((128, pairs), 1) // BS).astype(BF16)
    repeat = pairs // 128

    def square(flat):
        return jnp.dot(jnp.where(diag, flat, 0.0).astype(BF16), fold_minor, preferred_element_type=F32)

    occ_rep = jnp.dot(square(occ_row).astype(BF16), spread, preferred_element_type=F32)
    vir_rep = jnp.concatenate([square(vir_row)] * repeat, axis=1)

    nt = (((1,), (1,)), ((), ()))
    acc = jnp.zeros((BS, pairs), F32)
    lines = []
    for first in range(0, pairs, CHUNK):
        part = lax.dot_general(t_ref[0, first : first + CHUNK, :], adj_ref[...], nt, preferred_element_type=F32)
        gram = lax.dot_general(part.astype(BF16), t_ref[0], nt, preferred_element_type=F32)
        for at in range(CHUNK // BS):
            i = first // BS + at
            block_i = gram[at * BS : (at + 1) * BS, :]
            acc = acc + block_i * occ_rep[i : i + 1, :]
            lines.append(jnp.sum(block_i * vir_rep, axis=0, keepdims=True))
    zmat = jnp.concatenate(lines, axis=0)

    def flatten(mat, fold):
        high = mat.astype(BF16)
        low = (mat - high.astype(F32)).astype(BF16)
        both = jnp.dot(high, fold, preferred_element_type=F32) + jnp.dot(low, fold, preferred_element_type=F32)
        wide = jnp.concatenate([both] * repeat, axis=1)
        return jnp.sum(jnp.where(diag, wide, 0.0), axis=0, keepdims=True)

    occ_flat = flatten(zmat, fold_major)
    vir_flat = flatten(acc, fold_minor)
    slot = iota((own, pairs), 0)
    occ_out[row // own] = occ_out[row // own] + jnp.where(slot == row % own, occ_flat, 0.0)
    vir_acc[home] = vir_acc[home] + jnp.where(slot == block % own, vir_flat, 0.0)

    @pl.when(t == pl.num_programs(0) - 1)
    def _():
        vir_out[...] = vir_acc[...].astype(vir_out.dtype)


def tiles(sizes, rows, owners, blocks, occ, vir, adj, three, n_dev, n_aux):
    count, pairs, naux = three.shape
    own = occ.shape[0] // n_aux
    smem = pl.BlockSpec(memory_space=pltpu.SMEM)
    vmem = pl.BlockSpec(memory_space=pltpu.VMEM)
    return pl.pallas_call(
        functools.partial(tile_kernel, n_aux, own),
        grid=(count,),
        out_shape=(
            jax.ShapeDtypeStruct((n_aux, own, pairs), F32),
            jax.ShapeDtypeStruct((n_dev, own, pairs), BF16),
        ),
        in_specs=[smem] * 4 + [vmem] * 3 + [pl.BlockSpec((1, pairs, naux), lambda t: (t, 0, 0))],
        out_specs=(vmem, vmem),
        scratch_shapes=[pltpu.VMEM((n_dev, own, pairs), F32)],
        compiler_params=pltpu.CompilerParams(vmem_limit_bytes=48 * 1024 * 1024),
        name="tiles",
    )(sizes, rows, owners, blocks, occ, vir, adj, three)


def exchange_kernel(
    n_blk, n_aux, norm, sizes, occ_ref, vir_ref, occ_out, vir_out, occ_got, vir_got, occ_sems, vir_sems
):
    n_dev = n_blk * n_aux
    b = lax.axis_index("blk")
    a = lax.axis_index("aux")
    me = b * n_aux + a
    own, pairs = occ_out.shape
    barrier = pltpu.get_barrier_semaphore()

    def greet(k, carry):
        p = lax.rem(me + k, n_dev)
        pl.semaphore_signal(barrier, inc=1, device_id=(p // n_aux, p % n_aux), device_id_type=MESH)
        return carry

    lax.fori_loop(1, n_dev, greet, 0)
    pl.semaphore_wait(barrier, n_dev - 1)

    def vir_copy(k, source):
        p = lax.rem(me + k, n_dev)
        return pltpu.make_async_remote_copy(
            src_ref=vir_ref.at[p],
            dst_ref=vir_got.at[source],
            send_sem=vir_sems.at[0, k],
            recv_sem=vir_sems.at[1, source],
            device_id=(p // n_aux, p % n_aux),
            device_id_type=MESH,
        )

    def occ_copy(k, source):
        q = lax.rem(a + k, n_aux)
        return pltpu.make_async_remote_copy(
            src_ref=occ_ref.at[q],
            dst_ref=occ_got.at[source],
            send_sem=occ_sems.at[0, k],
            recv_sem=occ_sems.at[1, source],
            device_id=(b, q),
            device_id_type=MESH,
        )

    def start_vir(k, carry):
        vir_copy(k, me).start()
        return carry

    def start_occ(k, carry):
        occ_copy(k, a).start()
        return carry

    lax.fori_loop(1, n_dev, start_vir, 0)
    lax.fori_loop(1, n_aux, start_occ, 0)

    def take_vir(k, total):
        source = lax.rem(me + k, n_dev)
        vir_copy(k, source).wait_recv()
        return total + vir_got[source].astype(F32)

    def take_occ(k, total):
        source = lax.rem(a + k, n_aux)
        occ_copy(k, source).wait_recv()
        return total + occ_got[source]

    occ_sum = lax.fori_loop(1, n_aux, take_occ, occ_ref[a])
    vir_sum = lax.fori_loop(1, n_dev, take_vir, vir_ref[me].astype(F32))
    lane = iota((1, pairs), 1)
    for r in range(own):
        size = sizes[a * own + r]
        scale = jnp.where((lane // BS < size) & (lane % BS < size), norm, 0.0).astype(F32)
        occ_out[r : r + 1, :] = occ_sum[r : r + 1, :] * scale
        vir_out[r : r + 1, :] = vir_sum[r : r + 1, :] * scale

    def end_vir(k, carry):
        vir_copy(k, me).wait_send()
        return carry

    def end_occ(k, carry):
        occ_copy(k, a).wait_send()
        return carry

    lax.fori_loop(1, n_dev, end_vir, 0)
    lax.fori_loop(1, n_aux, end_occ, 0)


def exchange(sizes, occ, vir, n_blk, n_aux, norm):
    n_dev, own, pairs = vir.shape
    vmem = pl.BlockSpec(memory_space=pltpu.VMEM)
    out = jax.ShapeDtypeStruct((own, pairs), F32)
    return pl.pallas_call(
        functools.partial(exchange_kernel, n_blk, n_aux, norm),
        out_shape=(out, out),
        in_specs=[pl.BlockSpec(memory_space=pltpu.SMEM), vmem, vmem],
        out_specs=(vmem, vmem),
        scratch_shapes=[
            pltpu.VMEM(occ.shape, occ.dtype),
            pltpu.VMEM(vir.shape, vir.dtype),
            pltpu.SemaphoreType.DMA((2, n_aux)),
            pltpu.SemaphoreType.DMA((2, n_dev)),
        ],
        compiler_params=pltpu.CompilerParams(collective_id=1, has_side_effects=True),
        name="exchange",
    )(sizes, occ, vir)


def shards(
    n_blk, n_aux, adjoint, three_centre, occ_density, vir_density, block_sizes, tile_rows, col_owner, col_block
):
    n_dev = n_blk * n_aux
    count = three_centre.shape[0]
    naux = three_centre.shape[3]
    own = occ_density.shape[0] // n_aux
    depth = adjoint.shape[0]
    aux_here = lax.axis_index("aux")
    own_sizes = lax.dynamic_slice_in_dim(block_sizes, aux_here * own, own, 0)
    own_vir = lax.dynamic_slice_in_dim(vir_density, aux_here * own, own, 0)
    lane = jnp.arange(BS * BS, dtype=jnp.int32)[None, :]
    inside = (lane // BS < own_sizes[:, None]) & (lane % BS < own_sizes[:, None])
    own_vir = jnp.where(inside, own_vir, jnp.zeros_like(own_vir))
    got = gather(jnp.concatenate((adjoint, own_vir), axis=0), n_blk, n_aux)
    adj = got[:, :depth, :].reshape(naux, naux)
    vir = got[:, depth:, :]
    occ_terms, vir_terms = tiles(
        block_sizes, tile_rows, col_owner.reshape(count), col_block, occ_density, vir, adj,
        three_centre.reshape(count, BS * BS, naux), n_dev, n_aux,
    )
    return exchange(block_sizes, occ_terms, vir_terms, n_blk, n_aux, naux ** -0.5)


def solution(mesh):
    in_specs = (
        P(("blk", "aux"), None),
        P(("blk", "aux"), None, None, None),
        P("blk", None),
        P("blk", None),
        P("blk"),
        P(("blk", "aux")),
        P(("blk", "aux"), None),
        P(("blk", "aux")),
    )
    out_specs = (P(("blk", "aux"), None), P(("blk", "aux"), None))
    body = functools.partial(shards, mesh.shape["blk"], mesh.shape["aux"])
    return jax.shard_map(body, mesh=mesh, in_specs=in_specs, out_specs=out_specs, check_vma=False)
```

profile of v0, /device:TPU:0, one launch (start us, length us, event | category | flops | bytes accessed | tf_op | source)
XLA Modules:
  0.0 71.4 jit_solution(16676374292826512516)
XLA Ops:
  0.6 0.7 %dynamic_slice.6 = s32[2]{0:T(128)S(1)} dynamic-slice(s32[8]{0:T(128)} %sizes.3, s32[]{:T(128)S(6)} %select_n.31), dynamic_slice_sizes={2} | dynamic-slice | bytes 20 | tf_op jit(solution)/shard_map/dynamic_slice | solution.py:372
  1.4 0.8 %and_select_fusion = bf16[2,1024]{1,0:T(2,128)(2,1)S(1)} fusion(bf16[8,1024]{1,0:T(8,128)(2,1)} %param.11, s32[]{:T(128)S(6)} %select_n.31, s32[1024]{0:T(1024)S(1)} %get-tuple-element.6, s32[1024]{0:T(1024)S(1)} %get-tuple-element.7, s32[2]{0:T(128)S(1)} %dynamic_slice.6), kind=kLoop, calls=%fused_computation.1 | loop fusion | flops 8192 | bytes 16396 | tf_op jit(solution)/shard_map/jit(_where)/select_n | solution.py:376
  2.2 1.5 %pad_maximum_fusion.pay_ref = bf16[34,1024]{1,0:T(8,128)(2,1)} fusion(bf16[2,1024]{1,0:T(2,128)(2,1)S(1)} %and_select_fusion, bf16[32,1024]{1,0:T(8,128)(2,1)} %param.8), kind=kLoop, calls=%fused_computation | loop fusion | flops 139264 | bytes 139264 | tf_op jit(solution)/shard_map/concatenate | solution.py:377
  3.7 27.0 %gather.1 = bf16[32,34,1024]{2,1,0:T(8,128)(2,1)} custom-call(bf16[34,1024]{1,0:T(8,128)(2,1)} %pad_maximum_fusion.pay_ref), custom_call_target="tpu_custom_call" | custom-call | tf_op jit(solution)/shard_map/gather/pallas_call | solution.py:161
  30.7 0.0 copy-start.2
  30.7 0.0 copy-start.3
  30.7 0.0 copy-start.4
  30.7 0.0 copy-start.5
  30.7 0.0 copy-start.6
  30.8 1.1 %slice.6.vir_ref = bf16[32,2,1024]{2,1,0:T(2,128)(2,1)S(1)} slice(bf16[32,34,1024]{2,1,0:T(8,128)(2,1)} %gather.1), slice={[0:32], [32:34], [0:1024]} | slice | bytes 262144 | tf_op jit(solution)/shard_map/slice | solution.py:379
  31.9 1.9 %slice.7 = bf16[32,32,1024]{2,1,0:T(8,128)(2,1)S(1)} slice(bf16[32,34,1024]{2,1,0:T(8,128)(2,1)} %gather.1), slice={[0:32], [0:32], [0:1024]} | slice | bytes 4194304 | tf_op jit(solution)/shard_map/slice | solution.py:378
  33.8 0.0 copy-done.2
  33.8 0.0 copy-done.3
  33.8 0.0 copy-done.4
  33.8 0.0 copy-done.5
  33.8 0.0 copy-done.6
  33.8 22.9 %tiles.1 = (f32[4,2,1024]{2,1,0:T(2,128)S(1)}, bf16[32,2,1024]{2,1,0:T(2,128)(2,1)S(1)}) custom-call(s32[8]{0:T(128)S(1)} %copy-done.3, s32[4]{0:T(128)S(1)} %copy-done.4, s32[4]{0:T(128)S(1)} %bitcast.4, s32[4]{0:T(128)S(1)} %copy-done.6, bf16[8,1024]{1,0:T(8,128)(2,1)S(1)} %copy-done.2, bf16[32,2,1024]{2,1,0:T(2,128)(2,1)S(1)} %slice.6.vir_ref, ...), custom_call_target="tpu_custom_call" | custom-call | tf_op jit(solution)/shard_map/tiles/pallas_call | solution.py:246
  56.7 0.0 copy-start
  56.7 0.6 copy-done
  57.4 0.0 copy-start.1
  57.4 0.6 copy-done.1
  58.0 10.9 %exchange.1 = (f32[2,1024]{1,0:T(2,128)}, f32[2,1024]{1,0:T(2,128)}) custom-call(s32[8]{0:T(128)} %sizes.3, f32[4,2,1024]{2,1,0:T(2,128)} %copy-done.1, bf16[32,2,1024]{2,1,0:T(2,128)(2,1)} %copy-done), custom_call_target="tpu_custom_call" | custom-call | tf_op jit(solution)/shard_map/exchange/pallas_call | solution.py:347
  68.8 1.3 %copy.12 = f32[2,1024]{1,0:T(2,128)} copy(f32[2,1024]{1,0:T(2,128)} %get-tuple-element.10) | data formatting | bytes 16384
  70.1 1.3 %copy.13 = f32[2,1024]{1,0:T(2,128)} copy(f32[2,1024]{1,0:T(2,128)} %get-tuple-element.11) | data formatting | bytes 16384
  (1 shorter events, 0.0 us)
Async XLA Ops:
  30.7 3.1 %copy-start.2 = (bf16[8,1024]{1,0:T(8,128)(2,1)S(1)}, bf16[8,1024]{1,0:T(8,128)(2,1)}, u32[]{:S(2)}) copy-start(bf16[8,1024]{1,0:T(8,128)(2,1)} %occ_ref.1) | copy-start | bytes 49156
  30.7 3.1 %copy-start.3 = (s32[8]{0:T(128)S(1)}, s32[8]{0:T(128)}, u32[]{:S(2)}) copy-start(s32[8]{0:T(128)} %sizes.3) | copy-start | bytes 100
  30.7 3.1 %copy-start.4 = (s32[4]{0:T(128)S(1)}, s32[4]{0:T(128)}, u32[]{:S(2)}) copy-start(s32[4]{0:T(128)} %rows.1) | copy-start | bytes 52
  30.7 3.1 %copy-start.5 = (s32[4,1]{0,1:T(1,128)S(1)}, s32[4,1]{0,1:T(1,128)}, u32[]{:S(2)}) copy-start(s32[4,1]{0,1:T(1,128)} %param.14) | copy-start | bytes 52
  30.7 3.1 %copy-start.6 = (s32[4]{0:T(128)S(1)}, s32[4]{0:T(128)}, u32[]{:S(2)}) copy-start(s32[4]{0:T(128)} %blocks.1) | copy-start | bytes 52
  56.7 0.6 copy-start
  57.4 0.6 copy-start.1
where the time goes:
time: 71.9 us; the launch traced here: 71.4 us
  Pallas kernels  60.8 us (85%)
  local copies, waits for them, and re-layouts  7.59 us (11%)
  other arithmetic  2.28 us (3%)
  between operations  0.76 us (1%)
    pallas_call x1, Pallas kernels, gather(): pl.pallas_call(functools.partial(gather_kernel, n_blk // 2), out_shape=ja...  27 us
    pallas_call x1, Pallas kernels, tiles(): pl.pallas_call(functools.partial(tile_kernel, n_aux, own), grid=(count,),...  22.9 us
    pallas_call x1, Pallas kernels, exchange(): pl.pallas_call(functools.partial(exchange_kernel, n_blk, n_aux, norm), ou...  10.9 us
    unnamed x16, local copies, waits for them, and re-layouts  3.86 us
    slice x1, local copies, waits for them, and re-layouts, shards(): adj = got[:, :depth, :].reshape(naux, naux)  1.86 us
    concatenate x1, other arithmetic, shards(): got = gather(jnp.concatenate((adjoint, own_vir), axis=0), n_blk, n_aux)  1.49 us

commit v1 on v0

--- a/solution.py
+++ b/solution.py
@@ -18,7 +18,34 @@
     return lax.broadcasted_iota(jnp.int32, shape, dim)
 
 
-def gather_kernel(depth, pay_ref, out_ref, send_sem, recv_sem, own_sem):
+def fold(minor, pairs):
+    index = iota((pairs, 128), 0)
+    index = index % BS if minor else index // BS
+    return (index == iota((pairs, 128), 1) % BS).astype(BF16)
+
+
+def dot(left, right):
+    return jnp.dot(left, right, preferred_element_type=F32)
+
+
+def dot_nt(left, right):
+    return lax.dot_general(left, right, (((1,), (1,)), ((), ())), preferred_element_type=F32)
+
+
+def fused_kernel(
+    n_blk, n_aux, norm,
+    sizes, rows, owners, blocks, adj_ref, occ_ref, vir_ref, t_hbm,
+    occ_out, vir_out,
+    got, tbuf, cbuf, occ_rep, vir_rep, occ_sums, vir_sums, occ_send, vir_send, occ_got, vir_got,
+    t_sem, send_sem, recv_sem, occ_sems, vir_sems,
+):
+    n_dev = n_blk * n_aux
+    depth = n_blk // 2
+    count, pairs, naux = tbuf.shape
+    own = occ_out.shape[0]
+    arows = adj_ref.shape[0]
+    span = naux // depth
+    per_plane = n_dev // depth
     b = lax.axis_index("blk")
     a = lax.axis_index("aux")
     z, y, x, c = b // 2, b % 2, a // 2, a % 2
@@ -31,85 +58,123 @@
         mate: (b, x * 2 + 1 - c),
     }
     has_up, has_down = z < depth - 1, z > 0
+    me = b * n_aux + a
 
     def ident(xx, yy, zz, cc):
         return ((zz * 2 + yy) * 2 + xx) * 2 + cc
 
-    me = ident(x, y, z, c)
     barrier = pltpu.get_barrier_semaphore()
-    for way in (over_x, over_y, mate):
-        pl.semaphore_signal(barrier, inc=1, device_id=place[way], device_id_type=MESH)
-
-    @pl.when(has_up)
-    def _():
-        pl.semaphore_signal(barrier, inc=1, device_id=place[up], device_id_type=MESH)
-
-    @pl.when(has_down)
-    def _():
-        pl.semaphore_signal(barrier, inc=1, device_id=place[down], device_id_type=MESH)
-
-    own = pltpu.make_async_copy(pay_ref, out_ref.at[me], own_sem)
-    own.start()
-    pl.semaphore_wait(barrier, 3 + has_up.astype(jnp.int32) + has_down.astype(jnp.int32))
-
-    def copy(way, block, src=None):
+
+    def greet(k, carry):
+        p = lax.rem(me + k, n_dev)
+        pl.semaphore_signal(barrier, inc=1, device_id=(p // n_aux, p % n_aux), device_id_type=MESH)
+        return carry
+
+    lax.fori_loop(1, n_dev, greet, 0)
+    fetches = [pltpu.make_async_copy(t_hbm.at[t], tbuf.at[t], t_sem.at[t]) for t in range(count)]
+    for fetch in fetches:
+        fetch.start()
+
+    lane = iota((1, pairs), 1)
+    major, minor = lane // BS, lane % BS
+    got[me, :arows, :] = adj_ref[...]
+    vir_all = vir_ref[...].astype(F32)
+    slot = iota(vir_all.shape, 0)
+    mine = []
+    for r in range(own):
+        size = sizes[a * own + r]
+        row = jnp.sum(jnp.where(slot == a * own + r, vir_all, 0.0), axis=0, keepdims=True)
+        mine.append(jnp.where((major < size) & (minor < size), row, 0.0))
+    got[me, arows:, :] = jnp.concatenate(mine, axis=0).astype(BF16)
+
+    diag = iota((BS, pairs), 1) // BS == iota((BS, pairs), 0)
+    fold_minor = fold(True, pairs)
+    pl.semaphore_wait(barrier, n_dev - 1)
+
+    def copy(way, block):
         return pltpu.make_async_remote_copy(
-            src_ref=out_ref.at[block] if src is None else src,
-            dst_ref=out_ref.at[block],
+            src_ref=got.at[block],
+            dst_ref=got.at[block],
             send_sem=send_sem.at[way, block],
             recv_sem=recv_sem.at[block],
             device_id=place[way],
             device_id_type=MESH,
         )
 
-    def send(way, block, src=None, when=None):
+    def send(way, block, when=None):
         if when is None:
-            copy(way, block, src).start()
+            copy(way, block).start()
         else:
 
             @pl.when(when)
             def _():
-                copy(way, block, src).start()
+                copy(way, block).start()
 
     def arrive(block):
         copy(mate, block).wait_recv()
 
-    send(up, me, pay_ref, has_up)
-    send(down, me, pay_ref, has_down)
-    send(over_x, me, pay_ref)
-    send(over_y, me, pay_ref)
-    send(mate, me, pay_ref)
+    send(up, me, has_up)
+    send(down, me, has_down)
+    send(over_x, me)
+    send(over_y, me)
+    send(mate, me)
+
+    occ_all = occ_ref[...].astype(F32)
+    parts = []
+    for t in range(count):
+        size = sizes[rows[t]]
+        row = jnp.sum(jnp.where(slot == rows[t], occ_all, 0.0), axis=0, keepdims=True)
+        row = jnp.where((major < size) & (minor < size), row, 0.0)
+        parts.append(jnp.where(diag, row, 0.0))
+    spread = (iota((128, pairs), 0) == iota((128, pairs), 1) // BS).astype(BF16)
+    square = dot(jnp.concatenate(parts, axis=0).astype(BF16), fold_minor)
+    occ_rep[...] = dot(square.astype(BF16), spread).reshape(occ_rep.shape)
 
     def column(zz, from_up):
         block = ident(x, y, zz, c)
         arrive(block)
         if from_up:
-            send(down, block, when=has_down)
+            send(down, block, has_down)
         else:
-            send(up, block, when=has_up)
+            send(up, block, has_up)
         send(over_x, block)
         send(over_y, block)
         send(mate, block)
 
-    def sides(zz):
+    def sides(zz, _):
         block = ident(1 - x, y, zz, c)
         arrive(block)
-        send(over_y, block, when=zz % 2 == 0)
+        send(over_y, block, zz % 2 == 0)
         send(mate, block)
         block = ident(x, 1 - y, zz, c)
         arrive(block)
-        send(over_x, block, when=zz % 2 == 1)
+        send(over_x, block, zz % 2 == 1)
         send(mate, block)
 
-    def corner(zz):
+    def corner(zz, _):
         block = ident(1 - x, 1 - y, zz, c)
         arrive(block)
         send(mate, block)
 
+    def mates(zz, _):
+        for xx in (x, 1 - x):
+            for yy in (y, 1 - y):
+                arrive(ident(xx, yy, zz, 1 - c))
+
+    def contract(zz, first, last):
+        part = got[pl.ds(zz * per_plane, per_plane), :arows, :].reshape(span, naux)
+        columns = pl.ds(pl.multiple_of(zz * span, span), span)
+
+        def step(t, carry):
+            cbuf[t, :, columns] = dot_nt(tbuf[t], part).astype(BF16)
+            return carry
+
+        lax.fori_loop(first, last, step, 0)
+
     def planes(dist, work):
         if dist == 0:
             work(z, None)
-        elif 0 < dist < depth:
+        elif dist < depth:
 
             @pl.when(z + dist < depth)
             def _():
@@ -119,17 +184,85 @@
             def _():
                 work(z - dist, False)
 
-    for step in range(1, depth + 2):
-        planes(step, column)
-        planes(step - 1, lambda zz, _: sides(zz))
-        if step >= 2:
-            planes(step - 2, lambda zz, _: corner(zz))
-
-    own.wait()
-    for zz in range(depth):
-        for xx in (x, 1 - x):
-            for yy in (y, 1 - y):
-                arrive(ident(xx, yy, zz, 1 - c))
+    def whole(zz, _):
+        mates(zz, _)
+        contract(zz, 0, count)
+
+    planes(1, column)
+    planes(0, sides)
+    planes(2, column)
+    planes(1, sides)
+    planes(0, corner)
+    for fetch in fetches:
+        fetch.wait()
+    mates(z, None)
+    contract(z, 0, count // 2)
+    planes(3, column)
+    planes(1, corner)
+    planes(2, sides)
+    contract(z, count // 2, count)
+    for dist in range(1, depth):
+        planes(dist + 3, column)
+        planes(dist + 1, corner)
+        planes(dist + 2, sides)
+        planes(dist, whole)
+
+    parts = []
+    for t in range(count):
+        home = owners[t] * n_aux + blocks[t] // own
+        near = got[home, arows:, :].astype(F32)
+        row = jnp.sum(jnp.where(iota(near.shape, 0) == blocks[t] % own, near, 0.0), axis=0, keepdims=True)
+        parts.append(jnp.where(diag, row, 0.0))
+    square = dot(jnp.concatenate(parts, axis=0).astype(BF16), fold_minor)
+    vir_rep[...] = jnp.concatenate([square] * (pairs // 128), axis=1).reshape(vir_rep.shape)
+
+    def tile(t, carry):
+        acc = jnp.zeros((BS, pairs), F32)
+        lines = []
+        for first in range(0, pairs, CHUNK):
+            gram = dot_nt(cbuf[t, first : first + CHUNK, :], tbuf[t])
+            for at in range(CHUNK // BS):
+                i = first // BS + at
+                block_i = gram[at * BS : (at + 1) * BS, :]
+                acc = acc + block_i * occ_rep[t, i : i + 1, :]
+                lines.append(jnp.sum(block_i * vir_rep[t], axis=0, keepdims=True))
+        vir_sums[t] = acc
+        occ_sums[t] = jnp.concatenate(lines, axis=0)
+        return carry
+
+    lax.fori_loop(0, count, tile, 0)
+
+    def flatten(mat, folding):
+        high = mat.astype(BF16)
+        low = (mat - high.astype(F32)).astype(BF16)
+        both = dot(high, folding) + dot(low, folding)
+        lines = []
+        for t in range(count):
+            wide = jnp.concatenate([both[t * BS : (t + 1) * BS]] * (pairs // 128), axis=1)
+            lines.append(jnp.sum(jnp.where(diag, wide, 0.0), axis=0, keepdims=True))
+        return lines
+
+    vir_flat = flatten(vir_sums[...].reshape(count * BS, pairs), fold_minor)
+    shape = (n_dev, own, 1)
+    place_id = iota(shape, 0) * own + iota(shape, 1)
+    total = jnp.zeros(vir_send.shape, F32)
+    for t in range(count):
+        hot = (place_id == owners[t] * (n_aux * own) + blocks[t]).astype(F32)
+        total = total + hot * vir_flat[t].reshape(1, 1, pairs)
+    vir_send[...] = total.astype(BF16)
+    occ_flat = flatten(occ_sums[...].reshape(count * BS, pairs), fold(False, pairs))
+    shape = (n_aux, own, 1)
+    place_id = iota(shape, 0) * own + iota(shape, 1)
+    total = jnp.zeros(occ_send.shape, F32)
+    for t in range(count):
+        hot = (place_id == rows[t]).astype(F32)
+        total = total + hot * occ_flat[t].reshape(1, 1, pairs)
+    occ_send[...] = total
+
+    trade(
+        n_blk, n_aux, norm, sizes, occ_send, vir_send, occ_out, vir_out, occ_got, vir_got, occ_sems, vir_sems
+    )
+
     for zz in range(depth):
         block = ident(x, y, zz, c)
         for way in (over_x, over_y, mate):
@@ -154,23 +287,42 @@
         copy(mate, ident(1 - x, 1 - y, zz, c)).wait_send()
 
 
-def gather(payload, n_blk, n_aux):
+def fused(sizes, rows, owners, blocks, adj, occ, vir, three, n_blk, n_aux, norm):
     n_dev = n_blk * n_aux
-    if n_aux != 4 or n_blk % 2:
-        return lax.all_gather(payload, ("blk", "aux"), axis=0)
+    count, pairs, naux = three.shape
+    own = occ.shape[0] // n_aux
+    smem = pl.BlockSpec(memory_space=pltpu.SMEM)
+    vmem = pl.BlockSpec(memory_space=pltpu.VMEM)
+    out = jax.ShapeDtypeStruct((own, pairs), F32)
+    square = pltpu.VMEM((count, BS, pairs), F32)
     return pl.pallas_call(
-        functools.partial(gather_kernel, n_blk // 2),
-        out_shape=jax.ShapeDtypeStruct((n_dev,) + payload.shape, payload.dtype),
-        in_specs=[pl.BlockSpec(memory_space=pltpu.VMEM)],
-        out_specs=pl.BlockSpec(memory_space=pltpu.VMEM),
+        functools.partial(fused_kernel, n_blk, n_aux, norm),
+        out_shape=(out, out),
+        in_specs=[smem] * 4 + [vmem] * 3 + [pl.BlockSpec(memory_space=pl.ANY)],
+        out_specs=(vmem, vmem),
         scratch_shapes=[
+            pltpu.VMEM((n_dev, adj.shape[0] + own, naux), BF16),
+            pltpu.VMEM((count, pairs, naux), BF16),
+            pltpu.VMEM((count, pairs, naux), BF16),
+            square,
+            square,
+            square,
+            square,
+            pltpu.VMEM((n_aux, own, pairs), F32),
+            pltpu.VMEM((n_dev, own, pairs), BF16),
+            pltpu.VMEM((n_aux, own, pairs), F32),
+            pltpu.VMEM((n_dev, own, pairs), BF16),
+            pltpu.SemaphoreType.DMA((count,)),
             pltpu.SemaphoreType.DMA((5, n_dev)),
             pltpu.SemaphoreType.DMA((n_dev,)),
-            pltpu.SemaphoreType.DMA,
+            pltpu.SemaphoreType.DMA((2, n_aux)),
+            pltpu.SemaphoreType.DMA((2, n_dev)),
         ],
-        compiler_params=pltpu.CompilerParams(collective_id=0, has_side_effects=True),
-        name="gather",
-    )(payload)
+        compiler_params=pltpu.CompilerParams(
+            collective_id=0, has_side_effects=True, vmem_limit_bytes=50 * 1024 * 1024
+        ),
+        name="fused",
+    )(sizes, rows, owners, blocks, adj, occ, vir, three)
 
 
 def tile_kernel(
@@ -265,7 +417,6 @@
     b = lax.axis_index("blk")
     a = lax.axis_index("aux")
     me = b * n_aux + a
-    own, pairs = occ_out.shape
     barrier = pltpu.get_barrier_semaphore()
 
     def greet(k, carry):
@@ -275,6 +426,16 @@
 
     lax.fori_loop(1, n_dev, greet, 0)
     pl.semaphore_wait(barrier, n_dev - 1)
+
+    trade(n_blk, n_aux, norm, sizes, occ_ref, vir_ref, occ_out, vir_out, occ_got, vir_got, occ_sems, vir_sems)
+
+
+def trade(n_blk, n_aux, norm, sizes, occ_ref, vir_ref, occ_out, vir_out, occ_got, vir_got, occ_sems, vir_sems):
+    n_dev = n_blk * n_aux
+    b = lax.axis_index("blk")
+    a = lax.axis_index("aux")
+    me = b * n_aux + a
+    own, pairs = occ_out.shape
 
     def vir_copy(k, source):
         p = lax.rem(me + k, n_dev)
@@ -368,18 +529,24 @@
     naux = three_centre.shape[3]
     own = occ_density.shape[0] // n_aux
     depth = adjoint.shape[0]
+    three = three_centre.reshape(count, BS * BS, naux)
+    if n_aux == 4 and n_blk % 2 == 0:
+        return fused(
+            block_sizes, tile_rows, col_owner.reshape(count), col_block, adjoint, occ_density, vir_density,
+            three, n_blk, n_aux, naux ** -0.5,
+        )
     aux_here = lax.axis_index("aux")
     own_sizes = lax.dynamic_slice_in_dim(block_sizes, aux_here * own, own, 0)
     own_vir = lax.dynamic_slice_in_dim(vir_density, aux_here * own, own, 0)
     lane = jnp.arange(BS * BS, dtype=jnp.int32)[None, :]
     inside = (lane // BS < own_sizes[:, None]) & (lane % BS < own_sizes[:, None])
     own_vir = jnp.where(inside, own_vir, jnp.zeros_like(own_vir))
-    got = gather(jnp.concatenate((adjoint, own_vir), axis=0), n_blk, n_aux)
+    got = lax.all_gather(jnp.concatenate((adjoint, own_vir), axis=0), ("blk", "aux"), axis=0)
     adj = got[:, :depth, :].reshape(naux, naux)
     vir = got[:, depth:, :]
     occ_terms, vir_terms = tiles(
         block_sizes, tile_rows, col_owner.reshape(count), col_block, occ_density, vir, adj,
-        three_centre.reshape(count, BS * BS, naux), n_dev, n_aux,
+        three, n_dev, n_aux,
     )
     return exchange(block_sizes, occ_terms, vir_terms, n_blk, n_aux, naux ** -0.5)
 

time: 71.9 us -> 59.3 us (0.82)
  Pallas kernels: 60.8 us -> 52.2 us
  other arithmetic: 2.28 us -> 0 us
  local copies, waits for them, and re-layouts: 7.59 us -> 6.08 us
    pallas_call x3 -> x1, Pallas kernels: 60.8 us -> 52.2 us  [fused(): pl.pallas_call(functools.partial(fused_kernel, n_blk, n_aux, norm), out_s...]
    slice x2 -> x0, local copies, waits for them, and re-layouts: 3 us -> none  [the longest x1 1.86 us: shards(): adj = got[:, :depth, :].reshape(naux, naux)]
    unnamed x16, local copies, waits for them, and re-layouts: 3.86 us -> 6.08 us
    concatenate x1 -> x0, other arithmetic: 1.49 us -> none  [shards(): got = gather(jnp.concatenate((adjoint, own_vir), axis=0), n_blk, n_aux)]
    select_n x2 -> x0, other arithmetic: 0.8 us -> none  [the longest x1 0.79 us: shards(): own_vir = jnp.where(inside, own_vir, jnp.zeros_like(own_vir))]
    dynamic_slice x1 -> x0, local copies, waits for them, and re-layouts: 0.73 us -> none  [shards(): own_sizes = lax.dynamic_slice_in_dim(block_sizes, aux_here * own, own, 0)]
where the time goes in v1:
time: 59.3 us; the launch traced here: 58.9 us
  Pallas kernels  52.2 us (88%)
  local copies, waits for them, and re-layouts  6.08 us (10%)
  between operations  0.66 us (1%)
    pallas_call x1, Pallas kernels, fused(): pl.pallas_call(functools.partial(fused_kernel, n_blk, n_aux, norm), out_s...  52.2 us
    unnamed x16, local copies, waits for them, and re-layouts  6.08 us

profile of v1, /device:TPU:0, one launch (start us, length us, event | category | flops | bytes accessed | tf_op | source)
XLA Modules:
  0.0 58.9 jit_solution(9179432129793358018)
XLA Ops:
  0.6 0.0 copy-start
  0.6 0.8 %copy-done = bf16[32,1024]{1,0:T(8,128)(2,1)S(1)} copy-done((bf16[32,1024]{1,0:T(8,128)(2,1)S(1)}, bf16[32,1024]{1,0:T(8,128)(2,1)}, u32[]{:S(2)}) %copy-start) | copy-done | bytes 65560
  1.5 0.0 copy-start.1
  1.5 0.7 %copy-done.1 = bf16[8,1024]{1,0:T(8,128)(2,1)S(1)} copy-done((bf16[8,1024]{1,0:T(8,128)(2,1)S(1)}, bf16[8,1024]{1,0:T(8,128)(2,1)}, u32[]{:S(2)}) %copy-start.1) | copy-done | bytes 16408
  2.2 0.0 copy-start.2
  2.2 0.7 %copy-done.2 = bf16[8,1024]{1,0:T(8,128)(2,1)S(1)} copy-done((bf16[8,1024]{1,0:T(8,128)(2,1)S(1)}, bf16[8,1024]{1,0:T(8,128)(2,1)}, u32[]{:S(2)}) %copy-start.2) | copy-done | bytes 16408
  2.9 0.0 copy-start.3
  2.9 0.7 %copy-done.3 = s32[8]{0:T(128)S(1)} copy-done((s32[8]{0:T(128)S(1)}, s32[8]{0:T(128)}, u32[]{:S(2)}) %copy-start.3) | copy-done | bytes 56
  3.6 0.0 copy-start.4
  3.6 0.7 %copy-done.4 = s32[4]{0:T(128)S(1)} copy-done((s32[4]{0:T(128)S(1)}, s32[4]{0:T(128)}, u32[]{:S(2)}) %copy-start.4) | copy-done | bytes 40
  4.2 0.0 copy-start.5
  4.2 0.7 %copy-done.5 = s32[4,1]{0,1:T(1,128)S(1)} copy-done((s32[4,1]{0,1:T(1,128)S(1)}, s32[4,1]{0,1:T(1,128)}, u32[]{:S(2)}) %copy-start.5) | copy-done | bytes 40
  4.9 0.0 copy-start.6
  4.9 0.7 %copy-done.6 = s32[4]{0:T(128)S(1)} copy-done((s32[4]{0:T(128)S(1)}, s32[4]{0:T(128)}, u32[]{:S(2)}) %copy-start.6) | copy-done | bytes 40
  5.5 52.2 %fused.1 = (f32[2,1024]{1,0:T(2,128)S(1)}, f32[2,1024]{1,0:T(2,128)S(1)}) custom-call(s32[8]{0:T(128)S(1)} %copy-done.3, s32[4]{0:T(128)S(1)} %copy-done.4, s32[4]{0:T(128)S(1)} %bitcast.2, s32[4]{0:T(128)S(1)} %copy-done.6, bf16[32,1024]{1,0:T(8,128)(2,1)S(1)} %copy-done, bf16[8,1024]{1,0:T(8,128)(2,1)S(1)} %copy-done.1, bf16[8,1024]{1,0:T(8,128)(2,1)S(1)} %copy-done.2, ...), custom_call_target="tpu_custom_call" | custom-call | tf_op jit(solution)/shard_map/fused/pallas_call | solution.py:298
  57.7 0.6 %copy.12 = f32[2,1024]{1,0:T(2,128)} copy(f32[2,1024]{1,0:T(2,128)S(1)} %get-tuple-element.4) | data formatting | bytes 16384
  58.3 0.6 %copy.13 = f32[2,1024]{1,0:T(2,128)} copy(f32[2,1024]{1,0:T(2,128)S(1)} %get-tuple-element.5) | data formatting | bytes 16384
Async XLA Ops:
  0.6 0.8 %copy-start = (bf16[32,1024]{1,0:T(8,128)(2,1)S(1)}, bf16[32,1024]{1,0:T(8,128)(2,1)}, u32[]{:S(2)}) copy-start(bf16[32,1024]{1,0:T(8,128)(2,1)} %adj_ref.1) | copy-start | bytes 196612
  1.5 0.7 %copy-start.1 = (bf16[8,1024]{1,0:T(8,128)(2,1)S(1)}, bf16[8,1024]{1,0:T(8,128)(2,1)}, u32[]{:S(2)}) copy-start(bf16[8,1024]{1,0:T(8,128)(2,1)} %occ_ref.1) | copy-start | bytes 49156
  2.2 0.7 %copy-start.2 = (bf16[8,1024]{1,0:T(8,128)(2,1)S(1)}, bf16[8,1024]{1,0:T(8,128)(2,1)}, u32[]{:S(2)}) copy-start(bf16[8,1024]{1,0:T(8,128)(2,1)} %vir_ref.1) | copy-start | bytes 49156
  2.9 0.7 %copy-start.3 = (s32[8]{0:T(128)S(1)}, s32[8]{0:T(128)}, u32[]{:S(2)}) copy-start(s32[8]{0:T(128)} %sizes.1) | copy-start | bytes 100
  3.6 0.7 %copy-start.4 = (s32[4]{0:T(128)S(1)}, s32[4]{0:T(128)}, u32[]{:S(2)}) copy-start(s32[4]{0:T(128)} %rows.1) | copy-start | bytes 52
  4.2 0.7 %copy-start.5 = (s32[4,1]{0,1:T(1,128)S(1)}, s32[4,1]{0,1:T(1,128)}, u32[]{:S(2)}) copy-start(s32[4,1]{0,1:T(1,128)} %param.14) | copy-start | bytes 52
  4.9 0.7 %copy-start.6 = (s32[4]{0:T(128)S(1)}, s32[4]{0:T(128)}, u32[]{:S(2)}) copy-start(s32[4]{0:T(128)} %blocks.1) | copy-start | bytes 52

commit v2 on v1

--- a/solution.py
+++ b/solution.py
@@ -198,14 +198,12 @@
     mates(z, None)
     contract(z, 0, count // 2)
     planes(3, column)
-    planes(1, corner)
-    planes(2, sides)
     contract(z, count // 2, count)
     for dist in range(1, depth):
+        planes(dist, corner)
+        planes(dist + 1, sides)
+        planes(dist, whole)
         planes(dist + 3, column)
-        planes(dist + 1, corner)
-        planes(dist + 2, sides)
-        planes(dist, whole)
 
     parts = []
     for t in range(count):
@@ -319,7 +317,7 @@
             pltpu.SemaphoreType.DMA((2, n_dev)),
         ],
         compiler_params=pltpu.CompilerParams(
-            collective_id=0, has_side_effects=True, vmem_limit_bytes=50 * 1024 * 1024
+            collective_id=0, has_side_effects=True, vmem_limit_bytes=67043328
         ),
         name="fused",
     )(sizes, rows, owners, blocks, adj, occ, vir, three)

time: 59.3 us -> 55.8 us (0.941)
  local copies, waits for them, and re-layouts: 6.08 us -> 2.59 us
    unnamed x16 -> x2, local copies, waits for them, and re-layouts: 6.08 us -> 2.59 us
where the time goes in v2:
time: 55.8 us; the launch traced here: 55.5 us
  Pallas kernels  52.3 us (94%)
  local copies, waits for them, and re-layouts  2.59 us (5%)
  between operations  0.64 us (1%)
    pallas_call x1, Pallas kernels, fused(): pl.pallas_call(functools.partial(fused_kernel, n_blk, n_aux, norm), out_s...  52.3 us
    unnamed x2, local copies, waits for them, and re-layouts  2.59 us

profile of v2, /device:TPU:0, one launch (start us, length us, event | category | flops | bytes accessed | tf_op | source)
XLA Modules:
  0.0 55.5 jit_solution(12549606334442681869)
XLA Ops:
  0.6 52.3 %fused.1 = (f32[2,1024]{1,0:T(2,128)}, f32[2,1024]{1,0:T(2,128)}) custom-call(s32[8]{0:T(128)} %sizes.1, s32[4]{0:T(128)} %rows.1, s32[4]{0:T(128)} %bitcast.3, s32[4]{0:T(128)} %blocks.1, bf16[32,1024]{1,0:T(8,128)(2,1)} %adj_ref.1, bf16[8,1024]{1,0:T(8,128)(2,1)} %occ_ref.1, bf16[8,1024]{1,0:T(8,128)(2,1)} %vir_ref.1, bf16[4,1024,1024]{2,1,0:T(8,128)(2,1)} %bitcast.2), custom_call_target="tpu_custom_call" | custom-call | tf_op jit(solution)/shard_map/fused/pallas_call | solution.py:296
  52.9 1.3 %copy.12 = f32[2,1024]{1,0:T(2,128)} copy(f32[2,1024]{1,0:T(2,128)} %get-tuple-element.4) | data formatting | bytes 16384
  54.2 1.3 %copy.13 = f32[2,1024]{1,0:T(2,128)} copy(f32[2,1024]{1,0:T(2,128)} %get-tuple-element.5) | data formatting | bytes 16384

commit v3 on v2

--- a/solution.py
+++ b/solution.py
@@ -35,11 +35,12 @@
 def fused_kernel(
     n_blk, n_aux, norm,
     sizes, rows, owners, blocks, adj_ref, occ_ref, vir_ref, t_hbm,
-    occ_out, vir_out,
+    out_ref,
     got, tbuf, cbuf, occ_rep, vir_rep, occ_sums, vir_sums, occ_send, vir_send, occ_got, vir_got,
     t_sem, send_sem, recv_sem, occ_sems, vir_sems,
 ):
     n_dev = n_blk * n_aux
+    occ_out, vir_out = out_ref.at[0], out_ref.at[1]
     depth = n_blk // 2
     count, pairs, naux = tbuf.shape
     own = occ_out.shape[0]
@@ -291,13 +292,12 @@
     own = occ.shape[0] // n_aux
     smem = pl.BlockSpec(memory_space=pltpu.SMEM)
     vmem = pl.BlockSpec(memory_space=pltpu.VMEM)
-    out = jax.ShapeDtypeStruct((own, pairs), F32)
     square = pltpu.VMEM((count, BS, pairs), F32)
     return pl.pallas_call(
         functools.partial(fused_kernel, n_blk, n_aux, norm),
-        out_shape=(out, out),
+        out_shape=jax.ShapeDtypeStruct((2, own, pairs), F32),
         in_specs=[smem] * 4 + [vmem] * 3 + [pl.BlockSpec(memory_space=pl.ANY)],
-        out_specs=(vmem, vmem),
+        out_specs=vmem,
         scratch_shapes=[
             pltpu.VMEM((n_dev, adj.shape[0] + own, naux), BF16),
             pltpu.VMEM((count, pairs, naux), BF16),
@@ -529,10 +529,11 @@
     depth = adjoint.shape[0]
     three = three_centre.reshape(count, BS * BS, naux)
     if n_aux == 4 and n_blk % 2 == 0:
-        return fused(
+        both = fused(
             block_sizes, tile_rows, col_owner.reshape(count), col_block, adjoint, occ_density, vir_density,
             three, n_blk, n_aux, naux ** -0.5,
         )
+        return both[0], both[1]
     aux_here = lax.axis_index("aux")
     own_sizes = lax.dynamic_slice_in_dim(block_sizes, aux_here * own, own, 0)
     own_vir = lax.dynamic_slice_in_dim(vir_density, aux_here * own, own, 0)

time: 55.8 us -> 54.6 us (0.978)
  local copies, waits for them, and re-layouts: 2.59 us -> 1.32 us
    unnamed x2 -> x0, local copies, waits for them, and re-layouts: 2.59 us -> none
    squeeze x0 -> x1, local copies, waits for them, and re-layouts: none -> 1.32 us  [shards(): return (both[0], both[1])]
where the time goes in v3:
time: 54.6 us; the launch traced here: 54.4 us
  Pallas kernels  52.4 us (96%)
  local copies, waits for them, and re-layouts  1.32 us (2%)
  between operations  0.64 us (1%)
    pallas_call x1, Pallas kernels, fused(): pl.pallas_call(functools.partial(fused_kernel, n_blk, n_aux, norm), out_s...  52.4 us
    squeeze x1, local copies, waits for them, and re-layouts, shards(): return (both[0], both[1])  1.32 us

profile of v3, /device:TPU:0, one launch (start us, length us, event | category | flops | bytes accessed | tf_op | source)
XLA Modules:
  0.0 54.4 jit_solution(15237679386088295038)
XLA Ops:
  0.6 52.4 %fused.1 = f32[2,2,1024]{2,1,0:T(2,128)} custom-call(s32[8]{0:T(128)} %sizes.1, s32[4]{0:T(128)} %rows.1, s32[4]{0:T(128)} %bitcast.7, s32[4]{0:T(128)} %blocks.1, bf16[32,1024]{1,0:T(8,128)(2,1)} %adj_ref.1, bf16[8,1024]{1,0:T(8,128)(2,1)} %occ_ref.1, bf16[8,1024]{1,0:T(8,128)(2,1)} %vir_ref.1, bf16[4,1024,1024]{2,1,0:T(8,128)(2,1)} %bitcast.6), custom_call_target="tpu_custom_call" | custom-call | tf_op jit(solution)/shard_map/fused/pallas_call | solution.py:296
  53.1 1.3 %slice_bitcast_fusion = (f32[2,1024]{1,0:T(2,128)}, f32[2,1024]{1,0:T(2,128)}) fusion(f32[2,2,1024]{2,1,0:T(2,128)} %fused.1), kind=kLoop, calls=%fused_computation | loop fusion | bytes 32768 | tf_op jit(solution)/shard_map/squeeze | solution.py:536
